TPU v7x, 32 devices: a whole 2x2x4 slice. The times are simulated.
32 devices in a mesh: dp: 32 (over z, y, x, core).
Axes of the slice: x: 2, y: 2, z: 4, core: 2. Of those that a mesh axis runs over, the one named last changes fastest.
Arguments:
- block_in: bfloat16 [12608, 768], P('dp'), may hold values from -6 to 6
- slot_mask: int32 [12608], P('dp'), may hold values from 0 to 1, as said below
- gain_first: bfloat16 [768], P('dp'), may hold values from 0.5 to 1.5
- shift_first: bfloat16 [768], P('dp'), may hold values from -3 to 3
- packed_weight: bfloat16 [768, 2304], P('dp'), may hold values from -0.21875 to 0.21875
- query_bias: bfloat16 [768], P('dp'), may hold values from -3 to 3
- value_bias: bfloat16 [768], P('dp'), may hold values from -3 to 3
- out_weight: bfloat16 [768, 768], P('dp'), may hold values from -1.75 to 1.75
- out_bias: bfloat16 [768], P('dp'), may hold values from -3 to 3
- gain_second: bfloat16 [768], P('dp'), may hold values from 0.5 to 1.5
- shift_second: bfloat16 [768], P('dp'), may hold values from -3 to 3
- up_weight: bfloat16 [768, 3072], P('dp'), may hold values from -0.21875 to 0.21875
- up_bias: bfloat16 [3072], P('dp'), may hold values from -3 to 3
- down_weight: bfloat16 [3072, 768], P('dp'), may hold values from -0.109375 to 0.109375
- down_bias: bfloat16 [768], P('dp'), may hold values from -3 to 3
- cotangent: bfloat16 [12608, 768], P('dp'), may hold values from -6 to 6
Outputs:
- block_out: bfloat16 [12608, 768], P('dp')
- input_grad: float32 [12608, 768], P('dp')
- grad_gain_first: float32 [768], P('dp')
- grad_shift_first: float32 [768], P('dp')
- grad_packed_weight: float32 [768, 2304], P('dp')
- grad_query_bias: float32 [768], P('dp')
- grad_value_bias: float32 [768], P('dp')
- grad_out_weight: float32 [768, 768], P('dp')
- grad_out_bias: float32 [768], P('dp')
- grad_gain_second: float32 [768], P('dp')
- grad_shift_second: float32 [768], P('dp')
- grad_up_weight: float32 [768, 3072], P('dp')
- grad_up_bias: float32 [3072], P('dp')
- grad_down_weight: float32 [3072, 768], P('dp')
- grad_down_bias: float32 [768], P('dp')
Inputs may be any that keep to these rules, and one draw needn't show every extreme that they name: `slot_mask`: each image slot of 197 tokens is all ones or all zeros; on each device the live image slots come first; each device has at least 1 of its 2 image slots live, and some device has both live.
All inputs are finite; a program needn't handle non-finite values.
Results may differ from a plain program's by a relative error of at most 0.011.
Values may be sent and summed in bfloat16 or wider, within the bound.
No kernel may reach another device: no remote copies, remote signals or barrier semaphores. Data moves between devices by JAX's collectives and lax.ppermute only.
A program may use at most 192 MiB of HBM per device.

v0:
```python
import jax
import jax.numpy as jnp
from jax import lax
from jax.sharding import PartitionSpec as P

D = 768
HEADS = 12
HEAD_DIM = 64
LEN = 197


def layer_norm(values, gain, shift):
    centre_mean = jnp.mean(values, axis=-1, keepdims=True)
    centred = values - centre_mean
    variance = jnp.mean(centred * centred, axis=-1, keepdims=True)
    return centred * lax.rsqrt(variance + 1e-06) * gain + shift


def token_sum(values):
    return jnp.sum(values, axis=(0, 1), dtype=jnp.float32)


def shards(
    block_in,
    slot_mask,
    gain_first,
    shift_first,
    packed_weight,
    query_bias,
    value_bias,
    out_weight,
    out_bias,
    gain_second,
    shift_second,
    up_weight,
    up_bias,
    down_weight,
    down_bias,
    cotangent,
):
    f32 = jnp.float32
    bf16 = jnp.bfloat16
    scale = HEAD_DIM ** (-0.5)
    attn_full = (
        lax.all_gather(gain_first, "dp", axis=0, tiled=True),
        lax.all_gather(shift_first, "dp", axis=0, tiled=True),
        lax.all_gather(packed_weight, "dp", axis=0, tiled=True),
        lax.all_gather(query_bias, "dp", axis=0, tiled=True),
        lax.all_gather(value_bias, "dp", axis=0, tiled=True),
        lax.all_gather(out_weight, "dp", axis=0, tiled=True),
        lax.all_gather(out_bias, "dp", axis=0, tiled=True),
    )
    mlp_full = (
        lax.all_gather(gain_second, "dp", axis=0, tiled=True),
        lax.all_gather(shift_second, "dp", axis=0, tiled=True),
        lax.all_gather(up_weight, "dp", axis=0, tiled=True),
        lax.all_gather(up_bias, "dp", axis=0, tiled=True),
        lax.all_gather(down_weight, "dp", axis=0, tiled=True),
        lax.all_gather(down_bias, "dp", axis=0, tiled=True),
    )
    full_g1, full_c1, full_packed, full_qbias, full_vbias, full_out, full_obias = attn_full
    full_g2, full_c2, full_up, full_ubias, full_down, full_dbias = mlp_full
    images = block_in.shape[0] // LEN
    inputs = block_in.astype(f32).reshape(images, LEN, D)
    live = slot_mask.astype(f32).reshape(images, LEN, 1)
    normed_low = layer_norm(inputs, full_g1.astype(f32), full_c1.astype(f32)).astype(bf16)
    packed = jnp.einsum("gtd,de->gte", normed_low, full_packed, preferred_element_type=f32)
    packed = packed.reshape(images, LEN, 3, HEADS, HEAD_DIM)
    query = (packed[:, :, 0] + full_qbias.astype(f32).reshape(HEADS, HEAD_DIM)).astype(bf16)
    key_low = packed[:, :, 1].astype(bf16)
    value_low = (packed[:, :, 2] + full_vbias.astype(f32).reshape(HEADS, HEAD_DIM)).astype(bf16)
    scores = jnp.einsum("gqhe,gkhe->ghqk", query, key_low, preferred_element_type=f32) * scale
    top_score = jnp.max(scores, axis=-1, keepdims=True)
    log_total = top_score + jnp.log(jnp.sum(jnp.exp(scores - top_score), axis=-1, keepdims=True))
    attn_low = jnp.exp(scores - log_total).astype(bf16)
    mixed = jnp.einsum("ghqk,gkhe->gqhe", attn_low, value_low, preferred_element_type=f32)
    attended = mixed.astype(bf16).reshape(images, LEN, D)
    branch = jnp.einsum(
        "gtd,de->gte", attended, full_out, preferred_element_type=f32
    ) + full_obias.astype(f32)
    middle = inputs + branch
    normed_two = layer_norm(middle, full_g2.astype(f32), full_c2.astype(f32)).astype(bf16)
    pre_act = jnp.einsum(
        "gtd,df->gtf", normed_two, full_up, preferred_element_type=f32
    ) + full_ubias.astype(f32)
    gelu_exact = lambda values: jax.nn.gelu(values, approximate=False)
    activated_f, gelu_pull = jax.vjp(gelu_exact, pre_act)
    activated = activated_f.astype(bf16)
    mlp_out = jnp.einsum(
        "gtf,fd->gtd", activated, full_down, preferred_element_type=f32
    ) + full_dbias.astype(f32)
    block_out = ((middle + mlp_out) * live).astype(bf16).reshape(images * LEN, D)
    back_g2, back_up, back_down = (
        lax.all_gather(gain_second, "dp", axis=0, tiled=True),
        lax.all_gather(up_weight, "dp", axis=0, tiled=True),
        lax.all_gather(down_weight, "dp", axis=0, tiled=True),
    )
    d_res = cotangent.astype(f32).reshape(images, LEN, D) * live
    d_mlp = d_res.astype(bf16)
    grad_down_bias = token_sum(d_mlp)
    grad_down_weight = jnp.einsum("gtf,gtd->fd", activated, d_mlp, preferred_element_type=f32)
    d_act = jnp.einsum("gtd,fd->gtf", d_mlp, back_down, preferred_element_type=f32)
    d_pre = gelu_pull(d_act)[0].astype(bf16)
    grad_up_bias = token_sum(d_pre)
    grad_up_weight = jnp.einsum("gtd,gtf->df", normed_two, d_pre, preferred_element_type=f32)
    d_normed_two = jnp.einsum("gtf,df->gtd", d_pre, back_up, preferred_element_type=f32)
    zero_shift = jnp.zeros((D,), f32)
    norm_pull_two = jax.vjp(layer_norm, middle, back_g2.astype(f32), zero_shift)[1]
    d_mid_part, grad_gain_second, grad_shift_second = norm_pull_two(d_normed_two)
    d_middle = d_res + d_mid_part
    mlp_grads = (
        grad_gain_second,
        grad_shift_second,
        grad_up_weight,
        grad_up_bias,
        grad_down_weight,
        grad_down_bias,
    )
    back_g1, back_packed, back_out = (
        lax.all_gather(gain_first, "dp", axis=0, tiled=True),
        lax.all_gather(packed_weight, "dp", axis=0, tiled=True),
        lax.all_gather(out_weight, "dp", axis=0, tiled=True),
    )
    d_branch = d_middle.astype(bf16)
    grad_out_bias = token_sum(d_branch)
    grad_out_weight = jnp.einsum("gtd,gte->de", attended, d_branch, preferred_element_type=f32)
    d_att = jnp.einsum("gte,de->gtd", d_branch, back_out, preferred_element_type=f32)
    d_att = d_att.astype(bf16).reshape(images, LEN, HEADS, HEAD_DIM)
    again = jnp.einsum("gqhe,gkhe->ghqk", query, key_low, preferred_element_type=f32) * scale
    attn_again = jnp.exp(again - log_total)
    d_values = jnp.einsum("ghqk,gqhe->gkhe", attn_low, d_att, preferred_element_type=f32).astype(
        bf16
    )
    d_attn = jnp.einsum("gqhe,gkhe->ghqk", d_att, value_low, preferred_element_type=f32)
    d_scores = (
        attn_again * (d_attn - jnp.sum(attn_again * d_attn, axis=-1, keepdims=True))
    ).astype(bf16)
    d_query = (
        jnp.einsum("ghqk,gkhe->gqhe", d_scores, key_low, preferred_element_type=f32) * scale
    ).astype(bf16)
    d_keys = (
        jnp.einsum("ghqk,gqhe->gkhe", d_scores, query, preferred_element_type=f32) * scale
    ).astype(bf16)
    grad_query_bias = token_sum(d_query).reshape(D)
    grad_value_bias = token_sum(d_values).reshape(D)
    d_packed = jnp.stack([d_query, d_keys, d_values], axis=2).reshape(images, LEN, 3 * D)
    grad_packed_weight = jnp.einsum("gtd,gte->de", normed_low, d_packed, preferred_element_type=f32)
    d_normed = jnp.einsum("gte,de->gtd", d_packed, back_packed, preferred_element_type=f32)
    norm_pull_one = jax.vjp(layer_norm, inputs, back_g1.astype(f32), zero_shift)[1]
    d_in_part, grad_gain_first, grad_shift_first = norm_pull_one(d_normed)
    input_grad = (d_middle + d_in_part).reshape(images * LEN, D)
    attn_grads = (
        grad_gain_first,
        grad_shift_first,
        grad_packed_weight,
        grad_query_bias,
        grad_value_bias,
        grad_out_weight,
        grad_out_bias,
    )
    owned_all = lax.psum_scatter(attn_grads + mlp_grads, "dp", scatter_dimension=0, tiled=True)
    owned_attn = owned_all[:7]
    owned_mlp = owned_all[7:]
    return (block_out, input_grad) + tuple(owned_attn) + tuple(owned_mlp)


def solution(mesh):
    in_specs = (
        P("dp", None),
        P("dp"),
        P("dp"),
        P("dp"),
        P("dp", None),
        P("dp"),
        P("dp"),
        P("dp", None),
        P("dp"),
        P("dp"),
        P("dp"),
        P("dp", None),
        P("dp"),
        P("dp", None),
        P("dp"),
        P("dp", None),
    )
    out_specs = (
        P("dp", None),
        P("dp", None),
        P("dp"),
        P("dp"),
        P("dp", None),
        P("dp"),
        P("dp"),
        P("dp", None),
        P("dp"),
        P("dp"),
        P("dp"),
        P("dp", None),
        P("dp"),
        P("dp", None),
        P("dp"),
    )
    return jax.shard_map(shards, mesh=mesh, in_specs=in_specs, out_specs=out_specs, check_vma=False)
```

profile of v0, /device:TPU:0, one launch (start us, length us, event | category | flops | bytes accessed | tf_op | source)
XLA Modules:
  0.0 793.2 jit_solution(6325828315978471569)
XLA Ops:
  10.0 0.8 dynamic-update-slice
  12.6 0.8 dynamic-update-slice.3
  13.4 0.8 dynamic-update-slice.4
  16.7 0.8 dynamic-update-slice.7
  17.6 42.6 %all-reduce.19 = (bf16[768]{0:T(1024)(128)(2,1)S(1)}, bf16[768]{0:T(1024)(128)(2,1)S(1)}, bf16[768]{0:T(1024)(128)(2,1)S(1)}, bf16[768]{0:T(1024)(128)(2,1)S(1)}...) all-reduce(bf16[768]{0:T(1024)(128)(2,1)S(1)} %dynamic-update-slice, ...), channel_id=1, replica_groups=mesh['dp'=32] {'dp'}, use_global_device_ids=true, to_apply=%add.1 | all-reduce | flops 9216 | bytes 36864
  60.2 1.3 reshape.169
  62.3 1.0 reshape.198
  63.7 10.1 %all-gather.5.cloned.1.call-done = bf16[768,2304]{1,0:T(8,128)(2,1)} async-done(((bf16[24,2304]{1,0:T(8,128)(2,1)}), bf16[768,2304]{1,0:T(8,128)(2,1)}) %all-gather.5.cloned.1.call-update) | async-done | bytes 3538960 | tf_op jit(solution)/shard_map/all_gather | solution.py:47
  73.8 5.8 copy.51
  79.7 4.1 fusion.42
  83.7 0.9 multiply_reduce_fusion.1
  84.7 0.9 exponential_reduce_fusion
  85.8 1.5 copy-done
  87.4 1.1 convolution_convert_fusion.1
  88.5 41.3 %all-gather.7.cloned.1.call-done = bf16[768,768]{1,0:T(8,128)(2,1)} async-done(((bf16[24,768]{1,0:T(8,128)(2,1)}), bf16[768,768]{1,0:T(8,128)(2,1)}) %all-gather.7.cloned.1.call-update) | async-done | bytes 1179664 | tf_op jit(solution)/shard_map/all_gather | solution.py:50
  129.7 2.1 fusion.64
  131.8 1.1 copy-done.2
  133.2 62.1 %all-gather.9.cloned.1.call-done = bf16[768,3072]{1,0:T(8,128)(2,1)} async-done(((bf16[24,3072]{1,0:T(8,128)(2,1)}), bf16[768,3072]{1,0:T(8,128)(2,1)}) %all-gather.9.cloned.1.call-update) | async-done | bytes 4718608 | tf_op jit(solution)/shard_map/all_gather | solution.py:56
  195.2 6.4 fusion.38
  201.7 2.3 copy-done.9
  204.0 12.9 %multiply_convert_fusion.1 = (bf16[2,197,3072]{2,1,0:T(8,128)(2,1)}, f32[2,197,3072]{2,1,0:T(8,128)}) fusion(f32[2,197,3072]{2,1,0:T(8,128)S(1)} %get-tuple-element.56, f32[3072]{0:T(1024)S(1)} %convert_element_type.136, u8[197,3072]{1,0:T(8,128)(4,1)S(1)} %get-tuple-element.16, u8[197,3072]{1,0:T(8,128)(4,1)S(1)} %get-tuple-element.15), kind=kLoop, calls=%fused_computation.14 | loop fusion | flops 85936128 | bytes 13326336 | tf_op jit(solution)/shard_map/convert_element_type | solution.py:88
  216.8 43.7 %all-gather.11.cloned.1.call-done = bf16[3072,768]{1,0:T(8,128)(2,1)} async-done(((bf16[96,768]{1,0:T(8,128)(2,1)}), bf16[3072,768]{1,0:T(8,128)(2,1)}) %all-gather.11.cloned.1.call-update) | async-done | bytes 4718608 | tf_op jit(solution)/shard_map/all_gather | solution.py:58
  260.5 8.0 %convert_reduce_fusion = (f32[3072]{0:T(1024)S(1)}, bf16[2,197,3072]{2,1,0:T(8,128)(2,1)S(1)}) fusion(f32[2,197,3072]{2,1,0:T(8,128)} %get-tuple-element.47, bf16[3072,768]{1,0:T(8,128)(2,1)} %all-gather.11.cloned.1.call-done, f32[2,197,768]{2,1,0:T(8,128)S(1)} %reshape.172, f32[2,197]{1,0:T(2,128)S(1)} %mul.210, f32[2,197,3072]{2,1,0:T(8,128)} %copy-done.9, ...), kind=kOutput, calls=%fused_computation.10 | convolution fusion | flops 1880303616 | bytes 18058792 | tf_op jit(solution)/shard_map/gtd,fd->gtf/dot_general | solution.py:102
  268.6 5.7 multiply_reduce_fusion.2
  274.8 1.0 copy-done.5
  276.9 2.3 convolution_bitcast_fusion.3
  280.3 1.0 convert_element_type.125
  281.2 3.0 convolution_convert_fusion.2
  284.2 1.4 copy.54
  285.6 4.6 multiply_reduce_fusion
  290.3 1.1 multiply_convert_fusion
  291.6 0.9 fusion.36
  293.3 1.1 convert_reduce_fusion.1
  295.3 1.4 copy-done.14
  296.6 5.0 convolution_bitcast_fusion.2
  301.7 8.5 %convolution_bitcast_fusion.1 = f32[768,3072]{1,0:T(8,128)} fusion(bf16[2,197,3072]{2,1,0:T(8,128)(2,1)} %copy-done.18, f32[2,197,768]{2,1,0:T(8,128)} %copy-done.2, f32[768]{0:T(1024)S(1)} %convert_element_type.134, f32[768]{0:T(1024)S(1)} %convert_element_type.133, f32[2,197]{1,0:T(2,128)S(1)} %fusion.56, f32[2,197]{1,0:T(2,128)S(1)} %broadcast_multiply_fusion), kind=kOutput, calls=%fused_computation.2 | convolution fusion | flops 1860638208 | bytes 13077584 | tf_op jit(solution)/shard_map/gtd,gtf->df/dot_general | solution.py:105
  310.6 8.1 %convolution_bitcast_fusion = f32[3072,768]{1,0:T(8,128)} fusion(bf16[2,197,3072]{2,1,0:T(8,128)(2,1)} %get-tuple-element.46, f32[2,197,768]{2,1,0:T(8,128)S(1)} %reshape.172, f32[2,197]{1,0:T(2,128)S(1)} %mul.210), kind=kOutput, calls=%fused_computation.1 | convolution fusion | flops 1859730432 | bytes 13069864 | tf_op jit(solution)/shard_map/gtf,gtd->fd/dot_general | solution.py:101
  318.9 0.9 copy-done.13
  320.1 4.9 fusion.60
  325.0 1.0 copy-done.10
  326.6 40.7 %all-reduce.18 = (f32[768]{0:T(1024)S(1)}, f32[768]{0:T(1024)S(1)}, f32[768]{0:T(1024)S(1)}, f32[768]{0:T(1024)S(1)}, f32[768]{0:T(1024)S(1)}, /*index=5*/f32[76...) all-reduce(f32[768]{0:T(1024)S(1)} %get-tuple-element.17, ...), channel_id=2, replica_groups=mesh['dp'=32] {'dp'}, use_global_device_ids=true, to_apply=%region_12.0.clone | all-reduce | flops 9216 | bytes 73728
  372.0 3.2 add_add_fusion.2
  375.3 2.5 reshape.175
  377.8 5.2 fusion.33
  383.0 0.9 reshape.171
  384.5 118.1 %reduce-scatter.5.cloned.1.call-done = f32[24,2304]{1,0:T(8,128)} async-done(((f32[768,2304]{1,0:T(8,128)}), f32[24,2304]{1,0:T(8,128)}) %reduce-scatter.5.cloned.1.call-update) | async-done | bytes 221200 | tf_op jit(solution)/shard_map/reduce_scatter | solution.py:161
  502.6 141.1 %reduce-scatter.9.cloned.1.call-done = f32[24,3072]{1,0:T(8,128)} async-done(((f32[768,3072]{1,0:T(8,128)}), f32[24,3072]{1,0:T(8,128)}) %reduce-scatter.9.cloned.1.call-update) | async-done | bytes 294928 | tf_op jit(solution)/shard_map/reduce_scatter | solution.py:161
  643.7 142.4 %reduce-scatter.11.cloned.1.call-done = f32[96,768]{1,0:T(8,128)} async-done(((f32[3072,768]{1,0:T(8,128)}), f32[96,768]{1,0:T(8,128)}) %reduce-scatter.11.cloned.1.call-update) | async-done | bytes 294928 | tf_op jit(solution)/shard_map/reduce_scatter | solution.py:161
  (117 shorter events, 19.8 us)
Async XLA Ops:
  7.2 54.3 %copy-start.6 = (bf16[394,768]{1,0:T(8,128)(2,1)S(1)}, bf16[394,768]{1,0:T(8,128)(2,1)}, u32[]{:S(2)}) copy-start(bf16[394,768]{1,0:T(8,128)(2,1)} %param.16) | copy-start | bytes 1815556
  7.2 66.7 %all-gather.5.cloned.1.call-start = ((), (), s32[]{:S(2)}) async-start(), calls=%async_computation.4 | async-start | bytes 3649536 | tf_op jit(solution)/shard_map/all_gather | solution.py:47
  7.9 121.8 %all-gather.7.cloned.1.call-start = ((), (), s32[]{:S(2)}) async-start(), calls=%async_computation.5 | async-start | bytes 1216512 | tf_op jit(solution)/shard_map/all_gather | solution.py:50
  8.7 186.6 %all-gather.9.cloned.1.call-start = ((), (), s32[]{:S(2)}) async-start(), calls=%async_computation.6 | async-start | bytes 4866048 | tf_op jit(solution)/shard_map/all_gather | solution.py:56
  9.4 251.1 %all-gather.11.cloned.1.call-start = ((), (), s32[]{:S(2)}) async-start(), calls=%async_computation.7 | async-start | bytes 4866048 | tf_op jit(solution)/shard_map/all_gather | solution.py:58
  10.0 374.5 %reduce-scatter.7.cloned.1.call-start = ((), (), s32[]{:S(2)}) async-start(), calls=%async_computation.9 | async-start | bytes 2433024 | tf_op jit(solution)/shard_map/reduce_scatter | solution.py:161
  60.2 3.3 copy-start.17
  60.2 3.4 copy-start.12
  62.3 1.2 copy-start.7
  73.8 5.8 copy-start.16
  83.7 2.1 copy-start.1
  84.7 2.7 copy-start
  131.8 1.1 copy-start.2
  201.7 2.3 copy-start.9
  260.5 8.1 %copy-start.3 = (f32[2,197,768]{2,1,0:T(8,128)S(1)}, f32[2,197,768]{2,1,0:T(8,128)}, u32[]{:S(2)}) copy-start(f32[2,197,768]{2,1,0:T(8,128)} %copy-done.2) | copy-start | bytes 3631108
  268.5 5.7 copy-start.18
  274.8 1.0 copy-start.5
  276.1 0.8 copy-start.11
  279.2 1.1 copy-start.8
  279.2 223.4 %reduce-scatter.5.cloned.1.call-start = ((), (), s32[]{:S(2)}) async-start(), calls=%async_computation.8 | async-start | bytes 7299072 | tf_op jit(solution)/shard_map/reduce_scatter | solution.py:161
  285.6 4.7 slice-start
  285.6 4.7 slice-start.1
  285.6 5.8 slice-start.2
  290.3 1.4 slice-start.3
  295.0 1.7 copy-start.15
  295.3 1.4 copy-start.14
  301.7 342.0 %reduce-scatter.9.cloned.1.call-start = ((), (), s32[]{:S(2)}) async-start(), calls=%async_computation.10 | async-start | bytes 9732096 | tf_op jit(solution)/shard_map/reduce_scatter | solution.py:161
  310.3 475.8 %reduce-scatter.11.cloned.1.call-start = ((), (), s32[]{:S(2)}) async-start(), calls=%async_computation.11 | async-start | bytes 9732096 | tf_op jit(solution)/shard_map/reduce_scatter | solution.py:161
  318.7 1.1 copy-start.13
  325.0 1.0 copy-start.10
  375.3 2.5 copy-start.4
Sparse Core Ops, SparseCore 0:
  10.9 62.8 all-gather.4
  76.7 52.9 all-gather.6
  132.6 62.5 all-gather.8
  198.0 62.4 all-gather.10
  279.3 97.9 reduce-scatter.6
  384.4 118.1 reduce-scatter.4
  509.1 134.6 reduce-scatter.8
  651.2 134.8 reduce-scatter.10
where the time goes:
time: 803 us; the launch traced here: 793 us
  waiting for transfers between devices  561 us (70%)
  blocking collectives  83.3 us (10%)
  matrix products  72.7 us (9%)
  local copies, waits for them, and re-layouts  38.9 us (5%)
  other arithmetic  21.4 us (3%)
  between operations  14.8 us (2%)
    reduce_scatter x4, waiting for transfers between devices, shards(): lax.psum_scatter(attn_grads + mlp_grads, 'dp', scatter_dimension=0, tiled...  402 us
    unnamed x2, blocking collectives  83.3 us
    all_gather x1, waiting for transfers between devices, shards(): lax.all_gather(up_weight, 'dp', axis=0, tiled=True)  62.1 us
    all_gather x1, waiting for transfers between devices, shards(): lax.all_gather(down_weight, 'dp', axis=0, tiled=True)  43.7 us
    all_gather x1, waiting for transfers between devices, shards(): lax.all_gather(out_weight, 'dp', axis=0, tiled=True)  41.3 us
    unnamed x73, local copies, waits for them, and re-layouts  24.1 us
  transfers between devices with their start and end apart: 8, of which 7 were waited for; matrix products, arithmetic and copies ran while one was open for 13% of the time, Pallas kernels for 0%

commit v1 on v0

--- a/solution.py
+++ b/solution.py
@@ -7,6 +7,20 @@
 HEADS = 12
 HEAD_DIM = 64
 LEN = 197
+
+
+def weights_treat(row_data):
+    earlier = lax.axis_size("dp")
+    z1 = lax.axis_index("dp")
+    before, t_next = (earlier, z1)
+    wide_out, latest = (row_data, 1)
+    while latest < before:
+        y1 = lax.ppermute(wide_out, "dp", [(at, at ^ latest) for at in range(before)])
+        state_next = jnp.concatenate([wide_out, y1], axis=0)
+        work_now = jnp.concatenate([y1, wide_out], axis=0)
+        wide_out = jnp.where(t_next & latest == 0, state_next, work_now)
+        latest = 2 * latest
+    return wide_out
 
 
 def layer_norm(values, gain, shift):
@@ -53,7 +67,7 @@
     mlp_full = (
         lax.all_gather(gain_second, "dp", axis=0, tiled=True),
         lax.all_gather(shift_second, "dp", axis=0, tiled=True),
-        lax.all_gather(up_weight, "dp", axis=0, tiled=True),
+        weights_treat(up_weight),
         lax.all_gather(up_bias, "dp", axis=0, tiled=True),
         lax.all_gather(down_weight, "dp", axis=0, tiled=True),
         lax.all_gather(down_bias, "dp", axis=0, tiled=True),

time: 803 us -> 876 us (1.091)
  waiting for transfers between devices: 561 us -> 605 us
  blocking collectives: 83.3 us -> 98.9 us
  matrix products: 72.7 us -> 86 us
    all_gather x1, waiting for transfers between devices: 41.3 us -> 94.3 us  [shards(): lax.all_gather(out_weight, 'dp', axis=0, tiled=True)]
    ppermute x0 -> x5, waiting for transfers between devices: none -> 22.4 us  [weights_treat(): lax.ppermute(wide_out, 'dp', [(at, at ^ latest) for at in range(before)])]
    all_gather x1, waiting for transfers between devices: 62.1 us -> 45.2 us  [shards(): lax.all_gather(up_weight, 'dp', axis=0, tiled=True)]
    unnamed x2, blocking collectives: 83.3 us -> 98.9 us
    dot_general x1, matrix products: 8.04 us -> 20 us  [shards(): jnp.einsum('gtd,fd->gtf', d_mlp, back_down, preferred_element_type=f32)]
    all_gather x1, waiting for transfers between devices: 10.1 us -> 0.01 us  [shards(): lax.all_gather(packed_weight, 'dp', axis=0, tiled=True)]
    unnamed x73 -> x89, local copies, waits for them, and re-layouts: 24.1 us -> 17.9 us
  transfers between devices with their start and end apart: 8 -> 13, of which waited for: 7 -> 9; matrix products, arithmetic and copies ran while one was open for 13% -> 14% of each run, Pallas kernels for 0% -> 0%
where the time goes in v1:
time: 876 us; the launch traced here: 872 us
  waiting for transfers between devices  605 us (69%)
  blocking collectives  98.9 us (11%)
  matrix products  86 us (10%)
  local copies, waits for them, and re-layouts  31.5 us (4%)
  other arithmetic  27 us (3%)
  between operations  14.9 us (2%)
  starting transfers between devices  8.83 us (1%)
    reduce_scatter x4, waiting for transfers between devices, shards(): lax.psum_scatter(attn_grads + mlp_grads, 'dp', scatter_dimension=0, tiled...  401 us
    unnamed x2, blocking collectives  98.9 us
    all_gather x1, waiting for transfers between devices, shards(): lax.all_gather(out_weight, 'dp', axis=0, tiled=True)  94.3 us
    all_gather x1, waiting for transfers between devices, shards(): lax.all_gather(up_weight, 'dp', axis=0, tiled=True)  45.2 us
    all_gather x1, waiting for transfers between devices, shards(): lax.all_gather(down_weight, 'dp', axis=0, tiled=True)  39.7 us
    ppermute x5, waiting for transfers between devices, weights_treat(): lax.ppermute(wide_out, 'dp', [(at, at ^ latest) for at in range(before)])  22.4 us
    dot_general x1, matrix products, shards(): jnp.einsum('gtd,fd->gtf', d_mlp, back_down, preferred_element_type=f32)  20 us
    unnamed x89, local copies, waits for them, and re-layouts  17.9 us
  transfers between devices with their start and end apart: 13, of which 9 were waited for; matrix products, arithmetic and copies ran while one was open for 14% of the time, Pallas kernels for 0%

profile of v1, /device:TPU:0, one launch (start us, length us, event | category | flops | bytes accessed | tf_op | source)
XLA Modules:
  0.0 872.2 jit_solution(3928317394045998907)
XLA Ops:
  10.1 1.2 collective-permute-done
  11.3 1.0 maximum_select_fusion.4
  12.3 2.9 collective-permute-start.1
  15.2 7.3 collective-permute-done.1
  22.7 1.8 collective-permute-start.2
  24.5 13.9 %collective-permute-done.2 = bf16[96,3072]{1,0:T(8,128)(2,1)S(1)} collective-permute-done((bf16[96,3072]{1,0:T(8,128)(2,1)S(1)}, bf16[96,3072]{1,0:T(8,128)(2,1)S(1)}, u32[]{:S(2)}, u32[]{:S(2)}) %collective-permute-start.2) | collective-permute-done | bytes 589856 | tf_op jit(solution)/shard_map/ppermute | solution.py:18
  38.4 1.3 maximum_select_fusion.2
  39.6 1.5 collective-permute-start.3
  43.4 58.2 %all-reduce.19 = (bf16[768]{0:T(1024)(128)(2,1)S(1)}, bf16[768]{0:T(1024)(128)(2,1)S(1)}, bf16[768]{0:T(1024)(128)(2,1)S(1)}, bf16[768]{0:T(1024)(128)(2,1)S(1)}...) all-reduce(bf16[768]{0:T(1024)(128)(2,1)S(1)} %dynamic-update-slice, ...), channel_id=1, replica_groups=mesh['dp'=32] {'dp'}, use_global_device_ids=true, to_apply=%add.1 | all-reduce | flops 9216 | bytes 36864
  102.6 1.0 reshape.198
  104.0 3.8 maximum_select_fusion.1
  107.8 1.6 collective-permute-start.4
  109.4 5.8 copy.51
  115.2 4.1 fusion.52
  121.4 1.5 copy-done
  122.9 1.1 convolution_convert_fusion.1
  124.0 94.3 %all-gather.7.cloned.1.call-done = bf16[768,768]{1,0:T(8,128)(2,1)} async-done(((bf16[24,768]{1,0:T(8,128)(2,1)}), bf16[768,768]{1,0:T(8,128)(2,1)}) %all-gather.7.cloned.1.call-update) | async-done | bytes 1179664 | tf_op jit(solution)/shard_map/all_gather | solution.py:64
  218.4 2.1 fusion.75
  220.7 7.6 fusion.48
  228.4 2.3 copy-done.9
  230.6 12.2 %multiply_convert_fusion.1 = (bf16[2,197,3072]{2,1,0:T(8,128)(2,1)}, f32[2,197,3072]{2,1,0:T(8,128)}) fusion(f32[2,197,3072]{2,1,0:T(8,128)S(1)} %get-tuple-element.56, u8[197,3072]{1,0:T(8,128)(4,1)S(1)} %get-tuple-element.16, u8[197,3072]{1,0:T(8,128)(4,1)S(1)} %get-tuple-element.15), kind=kLoop, calls=%fused_computation.14 | loop fusion | flops 84725760 | bytes 13314048 | tf_op jit(solution)/shard_map/convert_element_type | solution.py:102
  242.9 39.7 %all-gather.9.cloned.1.call-done = bf16[3072,768]{1,0:T(8,128)(2,1)} async-done(((bf16[96,768]{1,0:T(8,128)(2,1)}), bf16[3072,768]{1,0:T(8,128)(2,1)}) %all-gather.9.cloned.1.call-update) | async-done | bytes 4718608 | tf_op jit(solution)/shard_map/all_gather | solution.py:72
  282.5 20.0 %convert_reduce_fusion = (f32[3072]{0:T(1024)S(1)}, bf16[2,197,3072]{2,1,0:T(8,128)(2,1)}) fusion(f32[2,197,3072]{2,1,0:T(8,128)} %get-tuple-element.47, f32[2,197,3072]{2,1,0:T(8,128)} %copy-done.9, bf16[3072,768]{1,0:T(8,128)(2,1)} %all-gather.9.cloned.1.call-done, f32[2,197,768]{2,1,0:T(8,128)S(1)} %reshape.172, f32[2,197]{1,0:T(2,128)S(1)} %mul.210), kind=kOutput, calls=%fused_computation.10 | convolution fusion | flops 1879093248 | bytes 18046504 | tf_op jit(solution)/shard_map/gtd,fd->gtf/dot_general | solution.py:116
  302.5 45.2 %all-gather.11.cloned.1.call-done = bf16[768,3072]{1,0:T(8,128)(2,1)} async-done(((bf16[24,3072]{1,0:T(8,128)(2,1)}), bf16[768,3072]{1,0:T(8,128)(2,1)}) %all-gather.11.cloned.1.call-update) | async-done | bytes 4718608 | tf_op jit(solution)/shard_map/all_gather | solution.py:109
  347.8 5.9 multiply_reduce_fusion.2
  354.2 1.0 copy-done.5
  356.3 2.2 convolution_bitcast_fusion.3
  358.6 1.0 copy-done.8
  359.6 1.0 convert_element_type.125
  360.6 3.0 convolution_convert_fusion.2
  363.6 1.4 copy.54
  365.0 4.6 multiply_reduce_fusion
  369.6 1.1 multiply_convert_fusion
  372.6 1.1 convert_reduce_fusion.1
  374.6 1.4 copy-done.14
  376.1 5.0 convolution_bitcast_fusion.2
  381.1 8.1 convolution_bitcast_fusion
  389.5 8.5 convolution_bitcast_fusion.1
  399.4 4.9 fusion.71
  404.4 1.1 copy-done.10
  406.0 40.7 %all-reduce.18 = (f32[768]{0:T(1024)S(1)}, f32[768]{0:T(1024)S(1)}, f32[768]{0:T(1024)S(1)}, f32[768]{0:T(1024)S(1)}, f32[768]{0:T(1024)S(1)}, /*index=5*/f32[76...) all-reduce(f32[768]{0:T(1024)S(1)} %get-tuple-element.17, ...), channel_id=2, replica_groups=mesh['dp'=32] {'dp'}, use_global_device_ids=true, to_apply=%region_12.13.clone | all-reduce | flops 9216 | bytes 73728
  451.4 3.3 add_add_fusion.2
  454.7 2.5 reshape.175
  457.3 5.2 fusion.43
  462.4 0.9 reshape.171
  464.0 117.8 %reduce-scatter.5.cloned.1.call-done = f32[24,2304]{1,0:T(8,128)} async-done(((f32[768,2304]{1,0:T(8,128)}), f32[24,2304]{1,0:T(8,128)}) %reduce-scatter.5.cloned.1.call-update) | async-done | bytes 221200 | tf_op jit(solution)/shard_map/reduce_scatter | solution.py:175
  581.8 141.2 %reduce-scatter.11.cloned.1.call-done = f32[96,768]{1,0:T(8,128)} async-done(((f32[3072,768]{1,0:T(8,128)}), f32[96,768]{1,0:T(8,128)}) %reduce-scatter.11.cloned.1.call-update) | async-done | bytes 294928 | tf_op jit(solution)/shard_map/reduce_scatter | solution.py:175
  723.0 142.1 %reduce-scatter.9.cloned.1.call-done = f32[24,3072]{1,0:T(8,128)} async-done(((f32[768,3072]{1,0:T(8,128)}), f32[24,3072]{1,0:T(8,128)}) %reduce-scatter.9.cloned.1.call-update) | async-done | bytes 294928 | tf_op jit(solution)/shard_map/reduce_scatter | solution.py:175
  (147 shorter events, 20.7 us)
Async XLA Ops:
  7.2 34.0 %copy-start.18 = (bf16[24]{0:T(256)(128)(2,1)S(1)}, bf16[24]{0:T(256)(128)(2,1)}, u32[]{:S(2)}) copy-start(bf16[24]{0:T(256)(128)(2,1)} %param.18) | copy-start | bytes 148
  7.2 34.3 %copy-start.19 = (bf16[24]{0:T(256)(128)(2,1)S(1)}, bf16[24]{0:T(256)(128)(2,1)}, u32[]{:S(2)}) copy-start(bf16[24]{0:T(256)(128)(2,1)} %param.19) | copy-start | bytes 148
  7.2 34.5 %copy-start.20 = (bf16[24]{0:T(256)(128)(2,1)S(1)}, bf16[24]{0:T(256)(128)(2,1)}, u32[]{:S(2)}) copy-start(bf16[24]{0:T(256)(128)(2,1)} %param.22) | copy-start | bytes 148
  7.2 34.7 %copy-start.21 = (bf16[24]{0:T(256)(128)(2,1)S(1)}, bf16[24]{0:T(256)(128)(2,1)}, u32[]{:S(2)}) copy-start(bf16[24]{0:T(256)(128)(2,1)} %param.21) | copy-start | bytes 148
  7.2 35.0 %copy-start.22 = (bf16[24]{0:T(256)(128)(2,1)S(1)}, bf16[24]{0:T(256)(128)(2,1)}, u32[]{:S(2)}) copy-start(bf16[24]{0:T(256)(128)(2,1)} %param.24) | copy-start | bytes 148
  7.2 35.2 %copy-start.23 = (bf16[24]{0:T(256)(128)(2,1)S(1)}, bf16[24]{0:T(256)(128)(2,1)}, u32[]{:S(2)}) copy-start(bf16[24]{0:T(256)(128)(2,1)} %param.25) | copy-start | bytes 148
  7.2 35.4 %copy-start.24 = (bf16[24]{0:T(256)(128)(2,1)S(1)}, bf16[24]{0:T(256)(128)(2,1)}, u32[]{:S(2)}) copy-start(bf16[24]{0:T(256)(128)(2,1)} %param.26) | copy-start | bytes 148
  7.3 35.6 %copy-start.25 = (bf16[24]{0:T(256)(128)(2,1)S(1)}, bf16[24]{0:T(256)(128)(2,1)}, u32[]{:S(2)}) copy-start(bf16[24]{0:T(256)(128)(2,1)} %param.30) | copy-start | bytes 148
  7.3 35.9 %copy-start.26 = (bf16[96]{0:T(256)(128)(2,1)S(1)}, bf16[96]{0:T(256)(128)(2,1)}, u32[]{:S(2)}) copy-start(bf16[96]{0:T(256)(128)(2,1)} %param.28) | copy-start | bytes 580
  7.3 94.3 %copy-start.6 = (bf16[394,768]{1,0:T(8,128)(2,1)S(1)}, bf16[394,768]{1,0:T(8,128)(2,1)}, u32[]{:S(2)}) copy-start(bf16[394,768]{1,0:T(8,128)(2,1)} %param.16) | copy-start | bytes 1815556
  7.3 102.1 %all-gather.5.cloned.1.call-start = ((), (), s32[]{:S(2)}) async-start(), calls=%async_computation.4 | async-start | bytes 3649536 | tf_op jit(solution)/shard_map/all_gather | solution.py:61
  8.0 210.3 %all-gather.7.cloned.1.call-start = ((), (), s32[]{:S(2)}) async-start(), calls=%async_computation.5 | async-start | bytes 1216512 | tf_op jit(solution)/shard_map/all_gather | solution.py:64
  8.8 273.8 %all-gather.9.cloned.1.call-start = ((), (), s32[]{:S(2)}) async-start(), calls=%async_computation.6 | async-start | bytes 4866048 | tf_op jit(solution)/shard_map/all_gather | solution.py:72
  9.5 338.3 %all-gather.11.cloned.1.call-start = ((), (), s32[]{:S(2)}) async-start(), calls=%async_computation.7 | async-start | bytes 4866048 | tf_op jit(solution)/shard_map/all_gather | solution.py:109
  9.5 1.7 collective-permute-start
  12.3 10.2 %collective-permute-start.1 = (bf16[48,3072]{1,0:T(8,128)(2,1)S(1)}, bf16[48,3072]{1,0:T(8,128)(2,1)S(1)}, u32[]{:S(2)}, u32[]{:S(2)}) collective-permute-start(bf16[48,3072]{1,0:T(8,128)(2,1)S(1)} %maximum_select_fusion.4), channel_id=1, source_target_pairs={{0,2},{1,3},{2,0},{3,1},{4,6},{5,7},{6,4},{7,5},{8,10},{9,11},{10,... | collective-permute-start | bytes 884744 | tf_op jit(solution)/shard_map/ppermute | solution.py:18
  22.7 15.7 %collective-permute-start.2 = (bf16[96,3072]{1,0:T(8,128)(2,1)S(1)}, bf16[96,3072]{1,0:T(8,128)(2,1)S(1)}, u32[]{:S(2)}, u32[]{:S(2)}) collective-permute-start(bf16[96,3072]{1,0:T(8,128)(2,1)S(1)} %maximum_select_fusion.3), channel_id=1, source_target_pairs={{0,4},{1,5},{2,6},{3,7},{4,0},{5,1},{6,2},{7,3},{8,12},{9,13},{10,... | collective-permute-start | bytes 1769480 | tf_op jit(solution)/shard_map/ppermute | solution.py:18
  39.6 64.4 %collective-permute-start.3 = (bf16[192,3072]{1,0:T(8,128)(2,1)}, bf16[192,3072]{1,0:T(8,128)(2,1)}, u32[]{:S(2)}, u32[]{:S(2)}) collective-permute-start(bf16[192,3072]{1,0:T(8,128)(2,1)} %maximum_select_fusion.2), channel_id=1, source_target_pairs={{0,8},{1,9},{2,10},{3,11},{4,12},{5,13},{6,14},{7,15},{8,0},{9,1},... | collective-permute-start | bytes 3538952 | tf_op jit(solution)/shard_map/ppermute | solution.py:18
  41.1 422.8 %reduce-scatter.7.cloned.1.call-start = ((), (), s32[]{:S(2)}) async-start(), calls=%async_computation.9 | async-start | bytes 2433024 | tf_op jit(solution)/shard_map/reduce_scatter | solution.py:175
  101.6 2.2 copy-start.17
  101.6 2.3 copy-start.12
  102.6 1.2 copy-start.7
  107.8 112.9 %collective-permute-start.4 = (bf16[384,3072]{1,0:T(8,128)(2,1)}, bf16[384,3072]{1,0:T(8,128)(2,1)}, u32[]{:S(2)}, u32[]{:S(2)}) collective-permute-start(bf16[384,3072]{1,0:T(8,128)(2,1)} %maximum_select_fusion.1), channel_id=1, source_target_pairs={{0,16},{1,17},{2,18},{3,19},{4,20},{5,21},{6,22},{7,23},{8,24},{9,... | collective-permute-start | bytes 7077896 | tf_op jit(solution)/shard_map/ppermute | solution.py:18
  109.4 5.8 copy-start.15
  119.3 2.1 copy-start.1
  120.2 2.7 copy-start
  220.4 7.9 copy-start.2
  228.4 2.3 copy-start.9
  347.8 5.9 copy-start.3
  354.2 1.0 copy-start.5
  355.5 0.8 copy-start.11
  358.5 1.1 copy-start.8
  358.6 223.2 %reduce-scatter.5.cloned.1.call-start = ((), (), s32[]{:S(2)}) async-start(), calls=%async_computation.8 | async-start | bytes 7299072 | tf_op jit(solution)/shard_map/reduce_scatter | solution.py:175
  364.9 4.7 slice-start
  364.9 4.7 slice-start.1
  365.0 5.8 slice-start.2
  369.6 1.4 slice-start.3
  374.3 1.7 copy-start.16
  374.6 1.4 copy-start.14
  381.1 341.9 %reduce-scatter.11.cloned.1.call-start = ((), (), s32[]{:S(2)}) async-start(), calls=%async_computation.11 | async-start | bytes 9732096 | tf_op jit(solution)/shard_map/reduce_scatter | solution.py:175
  389.3 475.9 %reduce-scatter.9.cloned.1.call-start = ((), (), s32[]{:S(2)}) async-start(), calls=%async_computation.10 | async-start | bytes 9732096 | tf_op jit(solution)/shard_map/reduce_scatter | solution.py:175
  398.0 1.1 copy-start.13
  404.4 1.1 copy-start.10
  454.7 2.5 copy-start.4
Sparse Core Ops, SparseCore 0:
  11.0 67.6 all-gather.4
  81.6 136.7 all-gather.6
  221.3 61.2 all-gather.8
  285.3 62.4 all-gather.10
  358.7 97.7 reduce-scatter.6
  463.5 118.2 reduce-scatter.4
  588.3 134.6 reduce-scatter.10
  730.5 134.6 reduce-scatter.8
